TPU v7x, 512 devices: a whole 4x8x8 slice. The times are simulated.
512 devices in a mesh: dom: 16 (over y, core), aux: 32 (over x, z).
Axes of the slice: x: 4, y: 8, z: 8, core: 2. Of those that a mesh axis runs over, the one named last changes fastest.
Arguments:
- integrals: bfloat16 [16, 1024, 512, 128], P('dom', 'aux'), may hold values from -0.25 to 0.25
- density: bfloat16 [16, 4, 128, 128], P('dom'), may hold values from -0.25 to 0.25
- dens_cols: int32 [16, 4], replicated, may hold values from 0 to 15, as said below
- neighbours: int32 [16, 4], replicated, may hold values from 0 to 15, as said below
- metric: bfloat16 [16, 1024, 1024], P('dom', 'aux'), may hold values from -0.5 to 2.5, as said below
Outputs:
- exchange: float32 [16, 128, 128], P('dom')
Inputs may be any that keep to these rules, and one draw needn't show every extreme that they name: `neighbours`: in each row the entries are distinct; position 0 holds the row's own block, the others are blocks within cyclic distance 2 of it, both blocks at distance 1 among them. `dens_cols`: in each row the entries are distinct; position 0 holds the row's own block, the others are blocks within cyclic distance 2 of it, both blocks at distance 1 among them. `metric`: each domain's matrix is symmetric.
All inputs are finite; a program needn't handle non-finite values.
Results may differ from a plain program's by a relative error of at most 0.004.
Values may be sent and summed in bfloat16 or wider, within the bound.
No kernel may reach another device: no remote copies, remote signals or barrier semaphores. Data moves between devices by JAX's collectives and lax.ppermute only.
A program may use at most 64 MiB of HBM per device.

v0:
```python
import jax
import jax.numpy as jnp
from jax import lax
from jax.sharding import PartitionSpec as P

RAD = 2


def passed_along(block, axis, distance):
    devices = range(lax.axis_size(axis))
    route = [((i - distance) % len(devices), i) for i in devices]
    return lax.ppermute(block, axis, route)


def body(integrals, density, dens_cols, neighbours, metric):
    domain_count = lax.axis_size("dom")
    my_domain = lax.axis_index("dom")
    block_size = density.shape[2]
    neigh_count = neighbours.shape[1]
    my_blocks = lax.dynamic_index_in_dim(neighbours, my_domain, 0, keepdims=False)
    slab_list = []
    for offset in range(-RAD, RAD + 1):
        if offset == 0:
            slab_list.append(density[0])
        else:
            slab_list.append(passed_along(density, "dom", -offset)[0])
    row_slabs = jnp.stack(slab_list)
    slot_index = (my_blocks - my_domain + RAD) % domain_count
    picked = jnp.take(row_slabs, slot_index, axis=0)
    tile_cols = jnp.take(dens_cols, my_blocks, axis=0)
    matches = (tile_cols[:, None, :] == my_blocks[None, :, None]).astype(jnp.bfloat16)
    dense_tiles = jnp.einsum("jsk,jkab->jasb", matches, picked, preferred_element_type=jnp.float32)
    density_local = dense_tiles.astype(jnp.bfloat16).reshape(
        neigh_count * block_size, neigh_count * block_size
    )
    half_product = jnp.einsum(
        "ls,plm->psm", density_local, integrals[0], preferred_element_type=jnp.float32
    ).astype(jnp.bfloat16)
    half_moved, ints_moved = (
        lax.all_to_all(half_product[None], "aux", split_axis=2, concat_axis=1, tiled=True),
        lax.all_to_all(integrals, "aux", split_axis=2, concat_axis=1, tiled=True),
    )
    columns = ints_moved[0].reshape(ints_moved.shape[1], -1)
    fitted = jnp.dot(
        lax.all_gather(metric, "aux", axis=1, tiled=True)[0],
        columns,
        preferred_element_type=jnp.float32,
    ).astype(jnp.bfloat16)
    fitted = fitted.reshape(half_moved.shape[1:])
    partial_value = jnp.einsum(
        "psm,psn->mn", half_moved[0], fitted, preferred_element_type=jnp.float32
    )
    summed = lax.psum(partial_value, "aux")
    return summed[None]


def solution(mesh):
    return jax.shard_map(
        body,
        mesh=mesh,
        in_specs=(
            P("dom", "aux", None, None),
            P("dom", None, None, None),
            P(),
            P(),
            P("dom", "aux", None),
        ),
        out_specs=P("dom", None, None),
        check_vma=False,
    )
```

profile of v0, /device:TPU:2, one launch (start us, length us, event | category | flops | bytes accessed | tf_op | source)
XLA Modules:
  0.0 421.5 jit_solution(17828483009210059733)
XLA Ops:
  6.5 6.9 %copy.30 = bf16[1,32,512,128]{3,1,0,2:T(8,128)(2,1)} copy(bf16[1,32,512,128]{3,2,1,0:T(8,128)(2,1)} %param.5) | data formatting | bytes 8388608 | tf_op args[0]
  13.4 13.7 %all-to-all-start.1 = ((bf16[1,32,512,128]{3,1,0,2:T(8,128)(2,1)}), bf16[1,32,512,128]{3,1,0,2:T(8,128)(2,1)}, u32[]{:S(2)}, u32[]{:S(2)}) async-start(bf16[1,32,512,128]{3,1,0,2:T(8,128)(2,1)} %copy.30), calls=%async_computation.1 | async-start | bytes 8388608 | tf_op jit(solution)/shard_map/all_to_all | solution.py:41
  27.1 3.5 collective-permute-start
  30.6 2.9 collective-permute-start.2
  33.5 2.6 collective-permute-start.3
  36.5 0.6 gather_fusion.1
  37.2 3.2 collective-permute-done.3
  40.4 0.6 gather_fusion
  41.2 0.5 convolution_convert_fusion
  41.8 4.6 %convert_bitcast_fusion.1 = bf16[1,32,512,128]{3,2,1,0:T(8,128)(2,1)S(1)} fusion(bf16[1,32,512,128]{3,2,1,0:T(8,128)(2,1)} %param.5, bf16[64,8,4,128]{3,2,1,0:T(4,128)(2,1)S(1)} %bitcast.62), kind=kOutput, calls=%fused_computation.8 | convolution fusion | flops 2149580800 | bytes 8912896 | tf_op jit(solution)/shard_map/ls,plm->psm/dot_general | solution.py:36
  46.3 4.6 %copy.27 = bf16[1,32,512,128]{3,1,0,2:T(8,128)(2,1)} copy(bf16[1,32,512,128]{3,2,1,0:T(8,128)(2,1)S(1)} %convert_bitcast_fusion.1) | data formatting | bytes 8388608 | tf_op jit(solution)/shard_map/broadcast_in_dim | solution.py:40
  51.0 70.6 %all-to-all-done.1 = bf16[1,32,512,128]{3,1,0,2:T(8,128)(2,1)} async-done(((bf16[1,32,512,128]{3,1,0,2:T(8,128)(2,1)}), bf16[1,32,512,128]{3,1,0,2:T(8,128)(2,1)}, u32[]{:S(2)}, u32[]{:S(2)}) %all-to-all-start.1) | async-done | bytes 4194336 | tf_op jit(solution)/shard_map/all_to_all | solution.py:41
  121.6 7.6 %all-to-all-start = ((bf16[1,32,512,128]{3,1,0,2:T(8,128)(2,1)}), bf16[1,32,512,128]{3,1,0,2:T(8,128)(2,1)}, u32[]{:S(2)}, u32[]{:S(2)}) async-start(bf16[1,32,512,128]{3,1,0,2:T(8,128)(2,1)} %copy.27), calls=%async_computation | async-start | bytes 8388608 | tf_op jit(solution)/shard_map/all_to_all | solution.py:40
  129.2 0.7 all-gather.2.cloned.1.call-update
  130.1 6.1 %copy.31 = bf16[1,32,32,16,128]{4,3,1,2,0:T(8,128)(2,1)} copy(bf16[1,32,32,16,128]{4,1,3,2,0:T(8,128)(2,1)} %bitcast.13) | data formatting | bytes 8388608 | tf_op jit(solution)/shard_map/all_to_all | solution.py:41
  136.2 106.2 %all-gather.2.cloned.1.call-done = bf16[1,1024,1024]{2,1,0:T(8,128)(2,1)} async-done(((bf16[1,32,1024]{2,1,0:T(8,128)(2,1)}), bf16[1,1024,1024]{2,1,0:T(8,128)(2,1)}) %all-gather.2.cloned.1.call-update) | async-done | bytes 2097168 | tf_op jit(solution)/shard_map/all_gather | solution.py:45
  242.4 7.3 %convert_bitcast_fusion = bf16[128,8,16,128]{3,1,2,0:T(8,128)(2,1)S(1)} fusion(bf16[128,8,16,128]{3,2,1,0:T(8,128)(2,1)} %bitcast.60, bf16[1,1024,1024]{2,1,0:T(8,128)(2,1)} %all-gather.2.cloned.1.call-done), kind=kOutput, calls=%fused_computation.7 | convolution fusion | flops 4297064448 | bytes 10485760 | tf_op jit(solution)/shard_map/dot_general | solution.py:44
  249.8 3.4 copy.37
  253.1 3.8 copy.28
  257.0 1.2 copy.29
  258.1 1.0 copy-done.1
  259.1 1.9 convolution_bitcast_fusion
  261.1 152.0 %all-reduce.2.cloned.1.call-done = f32[1,128,128]{2,1,0:T(8,128)} async-done(((f32[1,128,128]{2,1,0:T(8,128)}), f32[1,128,128]{2,1,0:T(8,128)}) %all-reduce.2.cloned.1.call-update) | async-done | bytes 65552 | tf_op jit(solution)/shard_map/psum | solution.py:53
  413.1 1.5 copy.55
  (28 shorter events, 0.9 us)
Async XLA Ops:
  6.5 29.7 %copy-start = (s32[16,4]{0,1:T(4,128)S(1)}, s32[16,4]{0,1:T(4,128)}, u32[]{:S(2)}) copy-start(s32[16,4]{0,1:T(4,128)} %param.8) | copy-start | bytes 772
  13.4 13.7 %copy-start.2 = (bf16[1,4,128,128]{3,2,1,0:T(8,128)(2,1)S(1)}, bf16[1,4,128,128]{3,2,1,0:T(8,128)(2,1)}, u32[]{:S(2)}) copy-start(bf16[1,4,128,128]{3,2,1,0:T(8,128)(2,1)} %param.6) | copy-start | bytes 393220
  13.4 22.7 %copy-start.3 = (s32[16,4]{0,1:T(4,128)S(1)}, s32[16,4]{0,1:T(4,128)}, u32[]{:S(2)}) copy-start(s32[16,4]{0,1:T(4,128)} %param.7) | copy-start | bytes 772
  13.4 108.2 %all-to-all-start.1 = ((bf16[1,32,512,128]{3,1,0,2:T(8,128)(2,1)}), bf16[1,32,512,128]{3,1,0,2:T(8,128)(2,1)}, u32[]{:S(2)}, u32[]{:S(2)}) async-start(bf16[1,32,512,128]{3,1,0,2:T(8,128)(2,1)} %copy.30), calls=%async_computation.1 | async-start | bytes 8388608 | tf_op jit(solution)/shard_map/all_to_all | solution.py:41
  27.1 10.0 %collective-permute-start = (bf16[1,4,128,128]{3,2,1,0:T(8,128)(2,1)S(1)}, bf16[1,4,128,128]{3,2,1,0:T(8,128)(2,1)S(1)}, u32[]{:S(2)}, u32[]{:S(2)}) collective-permute-start(bf16[1,4,128,128]{3,2,1,0:T(8,128)(2,1)S(1)} %copy-done.2), channel_id=1, source_target_pairs={{448,0},{480,32},{0,64},{32,96},{64,128},{96,160},{128,192},{160,2... | collective-permute-start | bytes 393224 | tf_op jit(solution)/shard_map/ppermute | solution.py:12
  30.6 6.6 %collective-permute-start.1 = (bf16[1,4,128,128]{3,2,1,0:T(8,128)(2,1)S(1)}, bf16[1,4,128,128]{3,2,1,0:T(8,128)(2,1)S(1)}, u32[]{:S(2)}, u32[]{:S(2)}) collective-permute-start(bf16[1,4,128,128]{3,2,1,0:T(8,128)(2,1)S(1)} %copy-done.2), channel_id=1, source_target_pairs={{480,0},{0,32},{32,64},{64,96},{96,128},{128,160},{160,192},{192,2... | collective-permute-start | bytes 393224 | tf_op jit(solution)/shard_map/ppermute | solution.py:12
  30.6 6.6 %collective-permute-start.2 = (bf16[1,4,128,128]{3,2,1,0:T(8,128)(2,1)S(1)}, bf16[1,4,128,128]{3,2,1,0:T(8,128)(2,1)S(1)}, u32[]{:S(2)}, u32[]{:S(2)}) collective-permute-start(bf16[1,4,128,128]{3,2,1,0:T(8,128)(2,1)S(1)} %copy-done.2), channel_id=1, source_target_pairs={{32,0},{64,32},{96,64},{128,96},{160,128},{192,160},{224,192},{256... | collective-permute-start | bytes 393224 | tf_op jit(solution)/shard_map/ppermute | solution.py:12
  33.5 6.8 %collective-permute-start.3 = (bf16[1,4,128,128]{3,2,1,0:T(8,128)(2,1)S(1)}, bf16[1,4,128,128]{3,2,1,0:T(8,128)(2,1)S(1)}, u32[]{:S(2)}, u32[]{:S(2)}) collective-permute-start(bf16[1,4,128,128]{3,2,1,0:T(8,128)(2,1)S(1)} %copy-done.2), channel_id=1, source_target_pairs={{64,0},{96,32},{128,64},{160,96},{192,128},{224,160},{256,192},{28... | collective-permute-start | bytes 393224 | tf_op jit(solution)/shard_map/ppermute | solution.py:12
  121.6 131.6 %all-to-all-start = ((bf16[1,32,512,128]{3,1,0,2:T(8,128)(2,1)}), bf16[1,32,512,128]{3,1,0,2:T(8,128)(2,1)}, u32[]{:S(2)}, u32[]{:S(2)}) async-start(bf16[1,32,512,128]{3,1,0,2:T(8,128)(2,1)} %copy.27), calls=%async_computation | async-start | bytes 8388608 | tf_op jit(solution)/shard_map/all_to_all | solution.py:40
  129.2 113.3 %all-gather.2.cloned.1.call-start = ((), (), s32[]{:S(2)}) async-start(), calls=%async_computation.2 | async-start | bytes 2162688 | tf_op jit(solution)/shard_map/all_gather | solution.py:45
  129.9 283.2 %all-reduce.2.cloned.1.call-start = ((), (), s32[]{:S(2)}) async-start(), calls=%async_computation.3 | async-start | bytes 131072 | tf_op jit(solution)/shard_map/psum | solution.py:53
  257.0 2.2 copy-start.1
Sparse Core Ops, SparseCore 0:
  133.1 109.2 all-gather.1
  261.2 151.8 all-reduce.1
where the time goes:
time: 422 us; the launch traced here: 421 us
  waiting for transfers between devices  333 us (79%)
  starting transfers between devices  30.5 us (7%)
  local copies, waits for them, and re-layouts  30 us (7%)
  matrix products  14.4 us (3%)
  between operations  13.6 us (3%)
    psum x1, waiting for transfers between devices, body(): summed = lax.psum(partial_value, 'aux')  152 us
    all_gather x1, waiting for transfers between devices, body(): lax.all_gather(metric, 'aux', axis=1, tiled=True)[0]  106 us
    all_to_all x1, waiting for transfers between devices, body(): lax.all_to_all(integrals, 'aux', split_axis=2, concat_axis=1, tiled=True)  70.6 us
    all_to_all x1, starting transfers between devices, body(): lax.all_to_all(integrals, 'aux', split_axis=2, concat_axis=1, tiled=True)  13.7 us
    unnamed x16, local copies, waits for them, and re-layouts  12.9 us
    ppermute x4, starting transfers between devices, passed_along(): return lax.ppermute(block, axis, route)  9.04 us
  transfers between devices with their start and end apart: 8, of which 4 were waited for; matrix products, arithmetic and copies ran while one was open for 7% of the time, Pallas kernels for 0%

commit v1 on v0

--- a/solution.py
+++ b/solution.py
@@ -50,7 +50,8 @@
     partial_value = jnp.einsum(
         "psm,psn->mn", half_moved[0], fitted, preferred_element_type=jnp.float32
     )
-    summed = lax.psum(partial_value, "aux")
+    shards = lax.all_gather(partial_value, "aux")
+    summed = jnp.sum(shards, axis=0)
     return summed[None]
 
 

time: 422 us -> 354 us (0.84)
  the two profiles are of different devices: /device:TPU:2 before, /device:TPU:8 now
where the time goes in v1:
time: 354 us; the launch traced here: 353 us
  waiting for transfers between devices  267 us (75%)
  local copies, waits for them, and re-layouts  28.5 us (8%)
  starting transfers between devices  27.6 us (8%)
  matrix products  14.4 us (4%)
  between operations  13.6 us (4%)
    all_gather x1, waiting for transfers between devices, body(): lax.all_gather(metric, 'aux', axis=1, tiled=True)[0]  107 us
    all_gather x1, waiting for transfers between devices, body(): shards = lax.all_gather(partial_value, 'aux')  82.5 us
    all_to_all x1, waiting for transfers between devices, body(): lax.all_to_all(integrals, 'aux', split_axis=2, concat_axis=1, tiled=True)  72.9 us
    all_to_all x1, starting transfers between devices, body(): lax.all_to_all(integrals, 'aux', split_axis=2, concat_axis=1, tiled=True)  13.4 us
    unnamed x15, local copies, waits for them, and re-layouts  11.4 us
    ppermute x4, starting transfers between devices, passed_along(): return lax.ppermute(block, axis, route)  8.79 us
    dot_general x1, matrix products, body(): jnp.dot(lax.all_gather(metric, 'aux', axis=1, tiled=True)[0], columns, pr...  7.32 us
  transfers between devices with their start and end apart: 8, of which 4 were waited for; matrix products, arithmetic and copies ran while one was open for 8% of the time, Pallas kernels for 0%

profile of v1, /device:TPU:8, one launch (start us, length us, event | category | flops | bytes accessed | tf_op | source)
XLA Modules:
  0.0 353.3 jit_solution(2800287532996315340)
XLA Ops:
  6.5 6.9 %copy.30 = bf16[1,32,512,128]{3,1,0,2:T(8,128)(2,1)} copy(bf16[1,32,512,128]{3,2,1,0:T(8,128)(2,1)} %param.5) | data formatting | bytes 8388608 | tf_op args[0]
  13.4 13.4 %all-to-all-start.1 = ((bf16[1,32,512,128]{3,1,0,2:T(8,128)(2,1)}), bf16[1,32,512,128]{3,1,0,2:T(8,128)(2,1)}, u32[]{:S(2)}, u32[]{:S(2)}) async-start(bf16[1,32,512,128]{3,1,0,2:T(8,128)(2,1)} %copy.30), calls=%async_computation.1 | async-start | bytes 8388608 | tf_op jit(solution)/shard_map/all_to_all | solution.py:41
  26.9 3.5 collective-permute-start
  30.4 1.7 collective-permute-start.2
  32.1 3.6 %collective-permute-start.3 = (bf16[1,4,128,128]{3,2,1,0:T(8,128)(2,1)S(1)}, bf16[1,4,128,128]{3,2,1,0:T(8,128)(2,1)S(1)}, u32[]{:S(2)}, u32[]{:S(2)}) collective-permute-start(bf16[1,4,128,128]{3,2,1,0:T(8,128)(2,1)S(1)} %copy-done.2), channel_id=1, source_target_pairs={{64,0},{96,32},{128,64},{160,96},{192,128},{224,160},{256,192},{28... | collective-permute-start | bytes 393224 | tf_op jit(solution)/shard_map/ppermute | solution.py:12
  36.0 0.6 gather_fusion.1
  36.8 3.6 %collective-permute-done.3 = bf16[1,4,128,128]{3,2,1,0:T(8,128)(2,1)S(1)} collective-permute-done((bf16[1,4,128,128]{3,2,1,0:T(8,128)(2,1)S(1)}, bf16[1,4,128,128]{3,2,1,0:T(8,128)(2,1)S(1)}, u32[]{:S(2)}, u32[]{:S(2)}) %collective-permute-start.3) | collective-permute-done | bytes 131104 | tf_op jit(solution)/shard_map/ppermute | solution.py:12
  40.4 0.6 gather_fusion
  41.1 0.5 convolution_convert_fusion
  41.7 4.6 %convert_bitcast_fusion.1 = bf16[1,32,512,128]{3,2,1,0:T(8,128)(2,1)S(1)} fusion(bf16[1,32,512,128]{3,2,1,0:T(8,128)(2,1)} %param.5, bf16[64,8,4,128]{3,2,1,0:T(4,128)(2,1)S(1)} %bitcast.64), kind=kOutput, calls=%fused_computation.8 | convolution fusion | flops 2149580800 | bytes 8912896 | tf_op jit(solution)/shard_map/ls,plm->psm/dot_general | solution.py:36
  46.3 4.6 %copy.27 = bf16[1,32,512,128]{3,1,0,2:T(8,128)(2,1)} copy(bf16[1,32,512,128]{3,2,1,0:T(8,128)(2,1)S(1)} %convert_bitcast_fusion.1) | data formatting | bytes 8388608 | tf_op jit(solution)/shard_map/broadcast_in_dim | solution.py:40
  50.9 72.9 %all-to-all-done.1 = bf16[1,32,512,128]{3,1,0,2:T(8,128)(2,1)} async-done(((bf16[1,32,512,128]{3,1,0,2:T(8,128)(2,1)}), bf16[1,32,512,128]{3,1,0,2:T(8,128)(2,1)}, u32[]{:S(2)}, u32[]{:S(2)}) %all-to-all-start.1) | async-done | bytes 4194336 | tf_op jit(solution)/shard_map/all_to_all | solution.py:41
  123.8 5.1 %all-to-all-start = ((bf16[1,32,512,128]{3,1,0,2:T(8,128)(2,1)}), bf16[1,32,512,128]{3,1,0,2:T(8,128)(2,1)}, u32[]{:S(2)}, u32[]{:S(2)}) async-start(bf16[1,32,512,128]{3,1,0,2:T(8,128)(2,1)} %copy.27), calls=%async_computation | async-start | bytes 8388608 | tf_op jit(solution)/shard_map/all_to_all | solution.py:40
  129.0 0.7 all-gather.4.cloned.1.call-update
  129.9 6.1 %copy.31 = bf16[1,32,32,16,128]{4,3,1,2,0:T(8,128)(2,1)} copy(bf16[1,32,32,16,128]{4,1,3,2,0:T(8,128)(2,1)} %bitcast.13) | data formatting | bytes 8388608 | tf_op jit(solution)/shard_map/all_to_all | solution.py:41
  136.0 107.0 %all-gather.4.cloned.1.call-done = bf16[1,1024,1024]{2,1,0:T(8,128)(2,1)} async-done(((bf16[1,32,1024]{2,1,0:T(8,128)(2,1)}), bf16[1,1024,1024]{2,1,0:T(8,128)(2,1)}) %all-gather.4.cloned.1.call-update) | async-done | bytes 2097168 | tf_op jit(solution)/shard_map/all_gather | solution.py:45
  243.0 7.3 %convert_bitcast_fusion = bf16[128,8,16,128]{3,1,2,0:T(8,128)(2,1)S(1)} fusion(bf16[128,8,16,128]{3,2,1,0:T(8,128)(2,1)} %bitcast.61, bf16[1,1024,1024]{2,1,0:T(8,128)(2,1)} %all-gather.4.cloned.1.call-done), kind=kOutput, calls=%fused_computation.7 | convolution fusion | flops 4297064448 | bytes 10485760 | tf_op jit(solution)/shard_map/dot_general | solution.py:44
  250.3 3.4 copy.37
  253.7 3.8 %copy.28 = bf16[1,32,512,128]{3,2,1,0:T(8,128)(2,1)S(1)} copy(bf16[1,32,512,128]{3,1,0,2:T(8,128)(2,1)} %all-to-all-done) | data formatting | bytes 8388608 | tf_op jit(solution)/shard_map/all_to_all | solution.py:40
  257.5 1.2 copy.29
  258.7 1.0 copy-done.1
  259.7 1.9 convolution_bitcast_fusion
  261.6 82.5 %all-gather.6.cloned.1.call-done = f32[4096,128]{1,0:T(8,128)} async-done(((f32[128,128]{1,0:T(8,128)}), f32[4096,128]{1,0:T(8,128)}) %all-gather.6.cloned.1.call-update) | async-done | bytes 2097168 | tf_op jit(solution)/shard_map/all_gather | solution.py:53
  344.1 2.3 reduce_sum.9
  (28 shorter events, 0.9 us)
Async XLA Ops:
  6.5 29.2 %copy-start = (s32[16,4]{0,1:T(4,128)S(1)}, s32[16,4]{0,1:T(4,128)}, u32[]{:S(2)}) copy-start(s32[16,4]{0,1:T(4,128)} %param.8) | copy-start | bytes 772
  13.4 13.4 %copy-start.2 = (bf16[1,4,128,128]{3,2,1,0:T(8,128)(2,1)S(1)}, bf16[1,4,128,128]{3,2,1,0:T(8,128)(2,1)}, u32[]{:S(2)}) copy-start(bf16[1,4,128,128]{3,2,1,0:T(8,128)(2,1)} %param.6) | copy-start | bytes 393220
  13.4 22.3 %copy-start.3 = (s32[16,4]{0,1:T(4,128)S(1)}, s32[16,4]{0,1:T(4,128)}, u32[]{:S(2)}) copy-start(s32[16,4]{0,1:T(4,128)} %param.7) | copy-start | bytes 772
  13.4 110.4 %all-to-all-start.1 = ((bf16[1,32,512,128]{3,1,0,2:T(8,128)(2,1)}), bf16[1,32,512,128]{3,1,0,2:T(8,128)(2,1)}, u32[]{:S(2)}, u32[]{:S(2)}) async-start(bf16[1,32,512,128]{3,1,0,2:T(8,128)(2,1)} %copy.30), calls=%async_computation.1 | async-start | bytes 8388608 | tf_op jit(solution)/shard_map/all_to_all | solution.py:41
  26.9 9.8 %collective-permute-start = (bf16[1,4,128,128]{3,2,1,0:T(8,128)(2,1)S(1)}, bf16[1,4,128,128]{3,2,1,0:T(8,128)(2,1)S(1)}, u32[]{:S(2)}, u32[]{:S(2)}) collective-permute-start(bf16[1,4,128,128]{3,2,1,0:T(8,128)(2,1)S(1)} %copy-done.2), channel_id=1, source_target_pairs={{448,0},{480,32},{0,64},{32,96},{64,128},{96,160},{128,192},{160,2... | collective-permute-start | bytes 393224 | tf_op jit(solution)/shard_map/ppermute | solution.py:12
  30.3 6.3 %collective-permute-start.1 = (bf16[1,4,128,128]{3,2,1,0:T(8,128)(2,1)S(1)}, bf16[1,4,128,128]{3,2,1,0:T(8,128)(2,1)S(1)}, u32[]{:S(2)}, u32[]{:S(2)}) collective-permute-start(bf16[1,4,128,128]{3,2,1,0:T(8,128)(2,1)S(1)} %copy-done.2), channel_id=1, source_target_pairs={{480,0},{0,32},{32,64},{64,96},{96,128},{128,160},{160,192},{192,2... | collective-permute-start | bytes 393224 | tf_op jit(solution)/shard_map/ppermute | solution.py:12
  30.4 6.4 %collective-permute-start.2 = (bf16[1,4,128,128]{3,2,1,0:T(8,128)(2,1)S(1)}, bf16[1,4,128,128]{3,2,1,0:T(8,128)(2,1)S(1)}, u32[]{:S(2)}, u32[]{:S(2)}) collective-permute-start(bf16[1,4,128,128]{3,2,1,0:T(8,128)(2,1)S(1)} %copy-done.2), channel_id=1, source_target_pairs={{32,0},{64,32},{96,64},{128,96},{160,128},{192,160},{224,192},{256... | collective-permute-start | bytes 393224 | tf_op jit(solution)/shard_map/ppermute | solution.py:12
  32.1 8.2 %collective-permute-start.3 = (bf16[1,4,128,128]{3,2,1,0:T(8,128)(2,1)S(1)}, bf16[1,4,128,128]{3,2,1,0:T(8,128)(2,1)S(1)}, u32[]{:S(2)}, u32[]{:S(2)}) collective-permute-start(bf16[1,4,128,128]{3,2,1,0:T(8,128)(2,1)S(1)} %copy-done.2), channel_id=1, source_target_pairs={{64,0},{96,32},{128,64},{160,96},{192,128},{224,160},{256,192},{28... | collective-permute-start | bytes 393224 | tf_op jit(solution)/shard_map/ppermute | solution.py:12
  123.8 129.8 %all-to-all-start = ((bf16[1,32,512,128]{3,1,0,2:T(8,128)(2,1)}), bf16[1,32,512,128]{3,1,0,2:T(8,128)(2,1)}, u32[]{:S(2)}, u32[]{:S(2)}) async-start(bf16[1,32,512,128]{3,1,0,2:T(8,128)(2,1)} %copy.27), calls=%async_computation | async-start | bytes 8388608 | tf_op jit(solution)/shard_map/all_to_all | solution.py:40
  128.9 114.0 %all-gather.4.cloned.1.call-start = ((), (), s32[]{:S(2)}) async-start(), calls=%async_computation.2 | async-start | bytes 2162688 | tf_op jit(solution)/shard_map/all_gather | solution.py:45
  129.7 214.4 %all-gather.6.cloned.1.call-start = ((), (), s32[]{:S(2)}) async-start(), calls=%async_computation.3 | async-start | bytes 2162688 | tf_op jit(solution)/shard_map/all_gather | solution.py:53
  257.5 2.2 copy-start.1
Sparse Core Ops, SparseCore 0:
  132.9 110.0 all-gather.3
  261.8 82.3 all-gather.5
